TPU v7x, 32 devices: a whole 2x2x4 slice. The times are simulated.
32 devices in a mesh: dp: 4 (over y, x), seq: 8 (over z, core).
Axes of the slice: x: 2, y: 2, z: 4, core: 2. Of those that a mesh axis runs over, the one named last changes fastest.
Arguments:
- inputs: bfloat16 [8, 1024, 1280], P('dp', 'seq'), may hold values from -6 to 6
- cotangent: bfloat16 [8, 1024, 1280], P('dp', 'seq'), may hold values from -6 to 6
- w_query: bfloat16 [1280, 1280], P(('dp', 'seq')), may hold values from -0.15625 to 0.15625
- w_key: bfloat16 [1280, 1280], P(('dp', 'seq')), may hold values from -0.15625 to 0.15625
- w_value: bfloat16 [1280, 1280], P(('dp', 'seq')), may hold values from -0.15625 to 0.15625
- w_out: bfloat16 [1280, 1280], P(('dp', 'seq')), may hold values from -1.25 to 1.25
- w_up: bfloat16 [1280, 1280], P(('dp', 'seq')), may hold values from -0.15625 to 0.15625
- w_down: bfloat16 [1280, 1280], P(('dp', 'seq')), may hold values from -0.15625 to 0.15625
- norm_attn: bfloat16 [1280], P(('dp', 'seq')), may hold values from 0.5 to 1.5
- norm_mlp: bfloat16 [1280], P(('dp', 'seq')), may hold values from 0.5 to 1.5
- query_scale: bfloat16 [1280], P(('dp', 'seq')), may hold values from 0 to 1.5
Outputs:
- output: bfloat16 [8, 1024, 1280], P('dp', 'seq')
- input_grad: float32 [8, 1024, 1280], P('dp', 'seq')
- grad_query: float32 [1280, 1280], P(('dp', 'seq'))
- grad_key: float32 [1280, 1280], P(('dp', 'seq'))
- grad_value: float32 [1280, 1280], P(('dp', 'seq'))
- grad_out: float32 [1280, 1280], P(('dp', 'seq'))
- grad_up: float32 [1280, 1280], P(('dp', 'seq'))
- grad_down: float32 [1280, 1280], P(('dp', 'seq'))
- grad_norm_attn: float32 [1280], P(('dp', 'seq'))
- grad_norm_mlp: float32 [1280], P(('dp', 'seq'))
- grad_query_scale: float32 [1280], P(('dp', 'seq'))
All inputs are finite; a program needn't handle non-finite values.
Results may differ from a plain program's by a relative error of at most 0.014.
Values may be sent and summed in bfloat16 or wider, within the bound.
No kernel may reach another device: no remote copies, remote signals or barrier semaphores. Data moves between devices by JAX's collectives and lax.ppermute only.
A program may use at most 320 MiB of HBM per device.

v0:
```python
import math

import jax
import jax.numpy as jnp
from jax import lax
from jax.sharding import PartitionSpec as P

H = 16


EPS = 1e-06
SOFT_BASE = 1.442695


def weight_outer(left, right):
    return lax.dot_general(
        left, right, (((0,), (0,)), ((), ())), preferred_element_type=jnp.float32
    )


def times_transpose(left, right):
    return lax.dot_general(
        left, right, (((1,), (1,)), ((), ())), preferred_element_type=jnp.float32
    )


def norm_back(grad, normed, inverse, gain):
    scaled = grad * gain
    inner = jnp.mean(scaled * normed, axis=-1, keepdims=True)
    return (inverse * (scaled - normed * inner), jnp.sum(grad * normed, axis=0))


def attend(q_low, k_low, v_low, first_row, num_heads):
    group_rows, model_width = q_low.shape
    head_size = model_width // num_heads
    query_heads = q_low.reshape(group_rows, num_heads, head_size)
    query_place = first_row + lax.iota(jnp.int32, group_rows)
    start_state = (
        jnp.full((num_heads, group_rows), -1e30, jnp.float32),
        jnp.zeros((num_heads, group_rows), jnp.float32),
        jnp.zeros((group_rows, model_width), jnp.float32),
    )
    key_piece = lax.all_gather(k_low, "seq", axis=0, tiled=True)
    value_piece = lax.all_gather(v_low, "seq", axis=0, tiled=True)
    count = key_piece.shape[0]

    def attend_compute(state):
        best, total, accum = state
        key_heads = key_piece.reshape(count, num_heads, head_size)
        value_heads = value_piece.reshape(count, num_heads, head_size)
        scores = jnp.einsum(
            "qhd,khd->hqk", query_heads, key_heads, preferred_element_type=jnp.float32
        )
        key_place = lax.iota(jnp.int32, count)
        allowed = (key_place[None, :] <= query_place[:, None])[None]
        scores = jnp.where(allowed, scores, -1e30)
        fresh = jnp.maximum(best, jnp.max(scores, axis=2))
        shrink = jnp.exp(best - fresh)
        probs = jnp.where(allowed, jnp.exp(scores - fresh[:, :, None]), 0.0)
        total = jnp.sum(probs, axis=2)
        mixed = jnp.einsum(
            "hqk,khd->qhd",
            probs.astype(jnp.bfloat16),
            value_heads,
            preferred_element_type=jnp.float32,
        )
        factor = jnp.repeat(shrink.T, head_size, axis=1)
        return (fresh, total, accum * factor + mixed.reshape(group_rows, model_width))

    best, total, accum = lax.cond(
        jnp.int32(0) > first_row + group_rows - 1, lambda state: state, attend_compute, start_state
    )
    mixed = accum / jnp.repeat(total.T, head_size, axis=1)
    return (mixed, best + jnp.log(total))


def query_grads(q_low, d_mixed, k_low, v_low, log_total, row_delta, first_row, num_heads):
    group_rows, model_width = q_low.shape
    head_size = model_width // num_heads
    query_heads = q_low.reshape(group_rows, num_heads, head_size)
    grad_heads = d_mixed.reshape(group_rows, num_heads, head_size)
    query_place = first_row + lax.iota(jnp.int32, group_rows)
    empty = jnp.zeros((group_rows, model_width), jnp.float32)
    key_piece = lax.all_gather(k_low, "seq", axis=0, tiled=True)
    value_piece = lax.all_gather(v_low, "seq", axis=0, tiled=True)
    count = key_piece.shape[0]

    def query_compute(accum):
        key_heads = key_piece.reshape(count, num_heads, head_size)
        value_heads = value_piece.reshape(count, num_heads, head_size)
        scores = jnp.einsum(
            "qhd,khd->hqk", query_heads, key_heads, preferred_element_type=jnp.float32
        )
        key_place = lax.iota(jnp.int32, count)
        allowed = (key_place[None, :] <= query_place[:, None])[None]
        probs = jnp.where(allowed, jnp.exp(scores - log_total[:, :, None]), 0.0)
        d_prob = jnp.einsum(
            "qhd,khd->hqk", grad_heads, value_heads, preferred_element_type=jnp.float32
        )
        d_score = (probs * (d_prob - row_delta[:, :, None])).astype(jnp.bfloat16)
        added = jnp.einsum("hqk,khd->qhd", d_score, key_heads, preferred_element_type=jnp.float32)
        return added.reshape(group_rows, model_width)

    return lax.cond(
        jnp.int32(0) > first_row + group_rows - 1, lambda accum: accum, query_compute, empty
    )


def key_grads(k_low, v_low, q_low, d_mixed, total_all, delta_all, first_row, num_heads):
    group_rows, model_width = k_low.shape
    head_size = model_width // num_heads
    key_heads = k_low.reshape(group_rows, num_heads, head_size)
    value_heads = v_low.reshape(group_rows, num_heads, head_size)
    key_place = first_row + lax.iota(jnp.int32, group_rows)
    empty = jnp.zeros((group_rows, model_width), jnp.float32)
    query_piece = lax.all_gather(q_low, "seq", axis=0, tiled=True)
    grad_piece = lax.all_gather(d_mixed, "seq", axis=0, tiled=True)
    count = query_piece.shape[0]

    def key_compute(state):
        query_heads = query_piece.reshape(count, num_heads, head_size)
        grad_heads = grad_piece.reshape(count, num_heads, head_size)
        scores = jnp.einsum(
            "qhd,khd->hqk", query_heads, key_heads, preferred_element_type=jnp.float32
        )
        query_place = lax.iota(jnp.int32, count)
        allowed = (key_place[None, :] <= query_place[:, None])[None]
        probs = jnp.where(allowed, jnp.exp(scores - total_all[:, :, None]), 0.0)
        d_prob = jnp.einsum(
            "qhd,khd->hqk", grad_heads, value_heads, preferred_element_type=jnp.float32
        )
        d_score = (probs * (d_prob - delta_all[:, :, None])).astype(jnp.bfloat16)
        more_values = jnp.einsum(
            "hqk,qhd->khd",
            probs.astype(jnp.bfloat16),
            grad_heads,
            preferred_element_type=jnp.float32,
        )
        more_keys = jnp.einsum(
            "hqk,qhd->khd", d_score, query_heads, preferred_element_type=jnp.float32
        )
        return (
            more_keys.reshape(group_rows, model_width),
            more_values.reshape(group_rows, model_width),
        )

    return lax.cond(
        jnp.int32(0) + count - 1 < first_row, lambda state: state, key_compute, (empty, empty)
    )


def per_device(
    inputs,
    cotangent,
    w_query,
    w_key,
    w_value,
    w_out,
    w_up,
    w_down,
    norm_attn,
    norm_mlp,
    query_scale,
):
    micro_count, group_rows, model_width = inputs.shape
    num_heads = H
    head_size = model_width // num_heads
    first_row = lax.axis_index("seq") * group_rows
    results = []
    in_grads = []
    totals = None
    for micro_index in range(micro_count):
        gathered = (
            lax.all_gather(w_query, ("dp", "seq"), axis=0, tiled=True),
            lax.all_gather(w_key, ("dp", "seq"), axis=0, tiled=True),
            lax.all_gather(w_value, ("dp", "seq"), axis=0, tiled=True),
            lax.all_gather(w_out, ("dp", "seq"), axis=0, tiled=True),
            lax.all_gather(w_up, ("dp", "seq"), axis=0, tiled=True),
            lax.all_gather(w_down, ("dp", "seq"), axis=0, tiled=True),
            lax.all_gather(norm_attn, ("dp", "seq"), axis=0, tiled=True),
            lax.all_gather(norm_mlp, ("dp", "seq"), axis=0, tiled=True),
            lax.all_gather(query_scale, ("dp", "seq"), axis=0, tiled=True),
        )
        full_query, full_key, full_value, full_out, full_up, full_down = gathered[:6]
        gain_attn = gathered[6].astype(jnp.float32)
        gain_mlp = gathered[7].astype(jnp.float32)
        scale_param = gathered[8].astype(jnp.float32)
        scale = jax.nn.softplus(scale_param) * (SOFT_BASE / math.sqrt(head_size))
        layer_in = inputs[micro_index].astype(jnp.float32)
        inv_attn = lax.rsqrt(jnp.mean(layer_in * layer_in, axis=-1, keepdims=True) + EPS)
        normed_attn = layer_in * inv_attn
        h_attn = (normed_attn * gain_attn).astype(jnp.bfloat16)
        q_raw = jnp.dot(h_attn, full_query, preferred_element_type=jnp.float32)
        q_low = (q_raw * scale).astype(jnp.bfloat16)
        k_low = jnp.dot(h_attn, full_key, preferred_element_type=jnp.float32).astype(jnp.bfloat16)
        v_low = jnp.dot(h_attn, full_value, preferred_element_type=jnp.float32).astype(jnp.bfloat16)
        mixed, log_total = attend(q_low, k_low, v_low, first_row, num_heads)
        attn_in = mixed.astype(jnp.bfloat16)
        resid = layer_in + jnp.dot(attn_in, full_out, preferred_element_type=jnp.float32)
        inv_mlp = lax.rsqrt(jnp.mean(resid * resid, axis=-1, keepdims=True) + EPS)
        normed_mlp = resid * inv_mlp
        h_mlp = (normed_mlp * gain_mlp).astype(jnp.bfloat16)
        up_proj = jnp.dot(h_mlp, full_up, preferred_element_type=jnp.float32)
        activated = jax.nn.silu(up_proj).astype(jnp.bfloat16)
        layer_out = resid + jnp.dot(activated, full_down, preferred_element_type=jnp.float32)
        results.append(layer_out.astype(jnp.bfloat16))
        regathered = (
            lax.all_gather(w_query, ("dp", "seq"), axis=0, tiled=True),
            lax.all_gather(w_key, ("dp", "seq"), axis=0, tiled=True),
            lax.all_gather(w_value, ("dp", "seq"), axis=0, tiled=True),
            lax.all_gather(w_out, ("dp", "seq"), axis=0, tiled=True),
            lax.all_gather(w_up, ("dp", "seq"), axis=0, tiled=True),
            lax.all_gather(w_down, ("dp", "seq"), axis=0, tiled=True),
        )
        back_query, back_key, back_value, back_out, back_up, back_down = regathered
        cotan_rows = cotangent[micro_index]
        cotan_float = cotan_rows.astype(jnp.float32)
        grad_down = weight_outer(activated, cotan_rows)
        d_act = times_transpose(cotan_rows, back_down)
        sigmoid_up = jax.nn.sigmoid(up_proj)
        d_up = (d_act * sigmoid_up * (1.0 + up_proj * (1.0 - sigmoid_up))).astype(jnp.bfloat16)
        grad_up = weight_outer(h_mlp, d_up)
        d_hmlp = times_transpose(d_up, back_up)
        d_norm_mlp, grad_gain_mlp = norm_back(d_hmlp, normed_mlp, inv_mlp, gain_mlp)
        d_resid = cotan_float + d_norm_mlp
        resid_low = d_resid.astype(jnp.bfloat16)
        grad_out = weight_outer(attn_in, resid_low)
        d_mixed = times_transpose(resid_low, back_out).astype(jnp.bfloat16)
        row_delta = jnp.sum(
            (d_mixed.astype(jnp.float32) * mixed).reshape(group_rows, num_heads, head_size), axis=2
        ).T
        total_all, delta_all = (
            lax.all_gather(log_total, "seq", axis=1, tiled=True),
            lax.all_gather(row_delta, "seq", axis=1, tiled=True),
        )
        d_qlow = query_grads(
            q_low, d_mixed, k_low, v_low, log_total, row_delta, first_row, num_heads
        )
        d_keys, d_values = key_grads(
            k_low, v_low, q_low, d_mixed, total_all, delta_all, first_row, num_heads
        )
        keys_low = d_keys.astype(jnp.bfloat16)
        values_low = d_values.astype(jnp.bfloat16)
        d_qraw = (d_qlow * scale).astype(jnp.bfloat16)
        grad_scale = (
            jnp.sum(d_qlow * q_raw, axis=0)
            * jax.nn.sigmoid(scale_param)
            * (SOFT_BASE / math.sqrt(head_size))
        )
        grad_query = weight_outer(h_attn, d_qraw)
        grad_key = weight_outer(h_attn, keys_low)
        grad_value = weight_outer(h_attn, values_low)
        d_hattn = (
            times_transpose(d_qraw, back_query)
            + times_transpose(keys_low, back_key)
            + times_transpose(values_low, back_value)
        )
        d_norm_attn, grad_gain_attn = norm_back(d_hattn, normed_attn, inv_attn, gain_attn)
        in_grads.append(d_resid + d_norm_attn)
        grad_part = (
            grad_query,
            grad_key,
            grad_value,
            grad_out,
            grad_up,
            grad_down,
            grad_gain_attn,
            grad_gain_mlp,
            grad_scale,
        )
        if totals is None:
            totals = tuple(grad_part)
        else:
            totals = tuple((earlier + later for earlier, later in zip(totals, grad_part)))
    totals = (
        lax.psum_scatter(totals[0], ("dp", "seq"), scatter_dimension=0, tiled=True),
        lax.psum_scatter(totals[1], ("dp", "seq"), scatter_dimension=0, tiled=True),
        lax.psum_scatter(totals[2], ("dp", "seq"), scatter_dimension=0, tiled=True),
        lax.psum_scatter(totals[3], ("dp", "seq"), scatter_dimension=0, tiled=True),
        lax.psum_scatter(totals[4], ("dp", "seq"), scatter_dimension=0, tiled=True),
        lax.psum_scatter(totals[5], ("dp", "seq"), scatter_dimension=0, tiled=True),
        lax.psum_scatter(totals[6], ("dp", "seq"), scatter_dimension=0, tiled=True),
        lax.psum_scatter(totals[7], ("dp", "seq"), scatter_dimension=0, tiled=True),
        lax.psum_scatter(totals[8], ("dp", "seq"), scatter_dimension=0, tiled=True),
    )
    return (
        jnp.stack(results),
        jnp.stack(in_grads),
        totals[0],
        totals[1],
        totals[2],
        totals[3],
        totals[4],
        totals[5],
        totals[6],
        totals[7],
        totals[8],
    )


def solution(mesh):
    placed = (
        P("dp", "seq", None),
        P("dp", "seq", None),
        P(("dp", "seq"), None),
        P(("dp", "seq"), None),
        P(("dp", "seq"), None),
        P(("dp", "seq"), None),
        P(("dp", "seq"), None),
        P(("dp", "seq"), None),
        P(("dp", "seq")),
        P(("dp", "seq")),
        P(("dp", "seq")),
    )
    return jax.shard_map(
        per_device,
        mesh=mesh,
        in_specs=placed,
        out_specs=(
            P("dp", "seq", None),
            P("dp", "seq", None),
            P(("dp", "seq"), None),
            P(("dp", "seq"), None),
            P(("dp", "seq"), None),
            P(("dp", "seq"), None),
            P(("dp", "seq"), None),
            P(("dp", "seq"), None),
            P(("dp", "seq")),
            P(("dp", "seq")),
            P(("dp", "seq")),
        ),
        check_vma=False,
    )
```

profile of v0, /device:TPU:0, one launch (start us, length us, event | category | flops | bytes accessed | tf_op | source)
XLA Modules:
  0.0 1553.4 jit_solution(6274619430469553487)
XLA Ops:
  12.0 42.2 %all-reduce.7 = (bf16[1280]{0:T(1024)(128)(2,1)S(1)}, bf16[1280]{0:T(1024)(128)(2,1)S(1)}, bf16[1280]{0:T(1024)(128)(2,1)S(1)}) all-reduce(bf16[1280]{0:T(1024)(128)(2,1)S(1)} %dynamic-update-slice, bf16[1280]{0:T(1024)(128)(2,1)S(1)} %dynamic-update-slice.1, ...), channel_id=1, replica_groups=mesh['dp'=4,'seq'=8] {'dp','seq'}, use_global_device_ids=true, to_apply=%add | all-reduce | flops 3840 | bytes 15360
  55.5 17.4 %all-gather.15.cloned.1.call-done = bf16[1280,1280]{1,0:T(8,128)(2,1)} async-done(((bf16[40,1280]{1,0:T(8,128)(2,1)}), bf16[1280,1280]{1,0:T(8,128)(2,1)}) %all-gather.15.cloned.1.call-update) | async-done | bytes 3276816 | tf_op jit(solution)/shard_map/all_gather | solution.py:175
  76.5 57.7 %all-gather.21.cloned.1.call-done = bf16[1280,1280]{1,0:T(8,128)(2,1)} async-done(((bf16[40,1280]{1,0:T(8,128)(2,1)}), bf16[1280,1280]{1,0:T(8,128)(2,1)}) %all-gather.21.cloned.1.call-update) | async-done | bytes 3276816 | tf_op jit(solution)/shard_map/all_gather | solution.py:176
  146.4 48.9 %all-gather.19.cloned.1.call-done = bf16[1280,1280]{1,0:T(8,128)(2,1)} async-done(((bf16[40,1280]{1,0:T(8,128)(2,1)}), bf16[1280,1280]{1,0:T(8,128)(2,1)}) %all-gather.19.cloned.1.call-update) | async-done | bytes 3276816 | tf_op jit(solution)/shard_map/all_gather | solution.py:174
  202.8 26.8 %all-gather.31.cloned.1.call-done = bf16[1024,1280]{1,0:T(8,128)(2,1)} async-done(((bf16[128,1280]{1,0:T(8,128)(2,1)}), bf16[1024,1280]{1,0:T(8,128)(2,1)}) %all-gather.31.cloned.1.call-update) | async-done | bytes 2621456 | tf_op jit(solution)/shard_map/all_gather | solution.py:43
  229.6 34.4 %all-gather.33.cloned.1.call-done = bf16[1024,1280]{1,0:T(8,128)(2,1)} async-done(((bf16[128,1280]{1,0:T(8,128)(2,1)}), bf16[1024,1280]{1,0:T(8,128)(2,1)}) %all-gather.33.cloned.1.call-update) | async-done | bytes 2621456 | tf_op jit(solution)/shard_map/all_gather | solution.py:44
  264.0 18.8 %conditional.7 = (f32[16,128]{1,0:T(8,128)S(1)}, f32[16,128]{1,0:T(8,128)S(1)}, f32[16,128]{1,0:T(8,128)S(1)}, f32[128,1280]{1,0:T(8,128)S(1)}) conditional(s32[]{:T(128)} %convert_element_type.190, (s32[128]{0:T(128)S(1)}, bf16[1024,1280]{1,0:T(8,128)(2,1)}, bf16[128,16,80]{0,2,1:T(8,128)(2,1)}, bf16[1024,1280]{1,0:T(8,128)(2,1)}) %tuple.181, () %tuple.67), branch_computations={%region_7.10_spmd, %region_10.11_spmd} | conditional | flops 692357120 | bytes 87835224 | solution.py:70
  284.8 13.0 all-gather.17.cloned.1.call-done
  297.8 35.1 %all-gather.23.cloned.1.call-done = bf16[1024,1280]{1,0:T(8,128)(2,1)} async-done(((bf16[128,1280]{1,0:T(8,128)(2,1)}), bf16[1024,1280]{1,0:T(8,128)(2,1)}) %all-gather.23.cloned.1.call-update) | async-done | bytes 2621456 | tf_op jit(solution)/shard_map/all_gather | solution.py:44
  332.9 18.9 %conditional.6 = (f32[16,128]{1,0:T(8,128)S(1)}, f32[16,128]{1,0:T(8,128)S(1)}, f32[16,128]{1,0:T(8,128)S(1)}, f32[128,1280]{1,0:T(8,128)S(1)}) conditional(s32[]{:T(128)} %convert_element_type.190, (s32[128]{0:T(128)S(1)}, bf16[1024,1280]{1,0:T(8,128)(2,1)}, bf16[128,16,80]{0,2,1:T(8,128)(2,1)}, bf16[1024,1280]{1,0:T(8,128)(2,1)}) %tuple.179, () %tuple.65), branch_computations={%region_1.4_spmd, %region_4.5_spmd} | conditional | flops 692357120 | bytes 87835224 | solution.py:70
  355.8 38.4 %all-gather.25.cloned.1.call-done = bf16[1280,1280]{1,0:T(8,128)(2,1)} async-done(((bf16[40,1280]{1,0:T(8,128)(2,1)}), bf16[1280,1280]{1,0:T(8,128)(2,1)}) %all-gather.25.cloned.1.call-update) | async-done | bytes 3276816 | tf_op jit(solution)/shard_map/all_gather | solution.py:177
  397.8 57.5 %all-gather.27.cloned.1.call-done = bf16[1280,1280]{1,0:T(8,128)(2,1)} async-done(((bf16[40,1280]{1,0:T(8,128)(2,1)}), bf16[1280,1280]{1,0:T(8,128)(2,1)}) %all-gather.27.cloned.1.call-update) | async-done | bytes 3276816 | tf_op jit(solution)/shard_map/all_gather | solution.py:178
  458.7 57.6 %all-gather.29.cloned.1.call-done = bf16[1280,1280]{1,0:T(8,128)(2,1)} async-done(((bf16[40,1280]{1,0:T(8,128)(2,1)}), bf16[1280,1280]{1,0:T(8,128)(2,1)}) %all-gather.29.cloned.1.call-update) | async-done | bytes 3276816 | tf_op jit(solution)/shard_map/all_gather | solution.py:179
  542.6 27.1 %conditional.10 = (f32[128,1280]{1,0:T(8,128)S(1)}) conditional(s32[]{:T(128)} %convert_element_type.190, (s32[128]{0:T(128)S(1)}, bf16[1024,1280]{1,0:T(8,128)(2,1)}, bf16[128,16,80]{0,2,1:T(8,128)(2,1)S(1)}, f32[16,128]{1,0:T(8,128)S(1)}, bf16[128,1280]{1,0:T(8,128)(2,1)S(1)}, /*index=5*/bf16[1024,1280]{1,0:T(8,128)(2,1)}, ...), branch_computations={%region_21.22_spmd, %region_22.23_spmd} | conditional | flops 1017249792 | bytes 38683144 | solution.py:104
  558.7 9.6 fusion.53
  569.7 29.4 %conditional.8 = (f32[128,1280]{1,0:T(8,128)}) conditional(s32[]{:T(128)} %convert_element_type.190, (s32[128]{0:T(128)S(1)}, bf16[1024,1280]{1,0:T(8,128)(2,1)}, bf16[128,16,80]{0,2,1:T(8,128)(2,1)}, f32[16,128]{1,0:T(8,128)S(1)}, bf16[128,1280]{1,0:T(8,128)(2,1)}, /*index=5*/bf16[1024,1280]{1,0:T(8,128)(2,1)}, ...), branch_computations={%region_14.15_spmd, %region_15.16_spmd} | conditional | flops 1017249792 | bytes 38683144 | solution.py:104
  587.4 9.6 fusion.32
  624.5 15.6 %all_gather.106 = f32[16,1024]{1,0:T(8,128)} all-gather(f32[16,128]{1,0:T(8,128)S(1)} %add.199), channel_id=1, replica_groups=mesh['dp'=4,'seq'=8] {'seq'}, dimensions={1}, use_global_device_ids=true | all-gather | bytes 73728 | tf_op jit(solution)/shard_map/all_gather | solution.py:233
  640.1 15.1 all_gather.108
  655.2 13.9 all_gather.102
  669.1 14.9 all_gather.104
  684.0 35.7 %conditional.11 = (bf16[128,1280]{0,1:T(8,128)(2,1)}, bf16[128,1280]{0,1:T(8,128)(2,1)}) conditional(s32[]{:T(128)} %convert_element_type.218, (s32[128]{0:T(128)S(1)}, bf16[1024,1280]{1,0:T(8,128)(2,1)}, bf16[128,1280]{1,0:T(8,128)(2,1)}, f32[16,1024]{1,0:T(8,128)}, bf16[1024,1280]{1,0:T(8,128)(2,1)}, /*index=5*/bf16[128,1280]{1,0:T(8,128)(2,1)}, ...), branch_computations={%region_23.24_spmd, %region_24.25_spmd} | conditional | flops 1359413248 | bytes 49349136 | solution.py:147
  703.4 9.9 fusion.68
  719.7 32.6 %conditional.9 = (bf16[128,1280]{0,1:T(8,128)(2,1)S(1)}, bf16[128,1280]{0,1:T(8,128)(2,1)S(1)}) conditional(s32[]{:T(128)} %convert_element_type.218, (s32[128]{0:T(128)S(1)}, bf16[1024,1280]{1,0:T(8,128)(2,1)}, bf16[128,1280]{1,0:T(8,128)(2,1)S(1)}, f32[16,1024]{1,0:T(8,128)S(1)}, bf16[1024,1280]{1,0:T(8,128)(2,1)}, ...), branch_computations={%region_16.17_spmd, %region_17.18_spmd} | conditional | flops 1359413248 | bytes 49349136 | solution.py:147
  725.1 6.5 fusion.157
  737.2 9.2 fusion.47
  783.6 39.6 %all-reduce.6 = (f32[1280]{0:T(1024)S(1)}, f32[1280]{0:T(1024)S(1)}, f32[1280]{0:T(1024)S(1)}) all-reduce(f32[1280]{0:T(1024)S(1)} %add.209, f32[1280]{0:T(1024)S(1)} %add.210, f32[1280]{0:T(1024)S(1)} %fusion.131), channel_id=8, replica_groups=mesh['dp'=4,'seq'=8] {'dp','seq'}, use_global_device_ids=true, to_apply=%region_34.35.clone | all-reduce | flops 3840 | bytes 30720
  827.6 125.6 %reduce-scatter.13.cloned.1.call-done = f32[40,1280]{1,0:T(8,128)} async-done(((f32[1280,1280]{1,0:T(8,128)}), f32[40,1280]{1,0:T(8,128)}) %reduce-scatter.13.cloned.1.call-update) | async-done | bytes 204816 | tf_op jit(solution)/shard_map/reduce_scatter | solution.py:279
  953.2 148.9 %reduce-scatter.15.cloned.1.call-done = f32[40,1280]{1,0:T(8,128)} async-done(((f32[1280,1280]{1,0:T(8,128)}), f32[40,1280]{1,0:T(8,128)}) %reduce-scatter.15.cloned.1.call-update) | async-done | bytes 204816 | tf_op jit(solution)/shard_map/reduce_scatter | solution.py:280
  1102.0 148.5 %reduce-scatter.17.cloned.1.call-done = f32[40,1280]{1,0:T(8,128)} async-done(((f32[1280,1280]{1,0:T(8,128)}), f32[40,1280]{1,0:T(8,128)}) %reduce-scatter.17.cloned.1.call-update) | async-done | bytes 204816 | tf_op jit(solution)/shard_map/reduce_scatter | solution.py:281
  1250.5 148.3 %reduce-scatter.9.cloned.1.call-done = f32[40,1280]{1,0:T(8,128)} async-done(((f32[1280,1280]{1,0:T(8,128)}), f32[40,1280]{1,0:T(8,128)}) %reduce-scatter.9.cloned.1.call-update) | async-done | bytes 204816 | tf_op jit(solution)/shard_map/reduce_scatter | solution.py:277
  1398.8 147.6 %reduce-scatter.11.cloned.1.call-done = f32[40,1280]{1,0:T(8,128)} async-done(((f32[1280,1280]{1,0:T(8,128)}), f32[40,1280]{1,0:T(8,128)}) %reduce-scatter.11.cloned.1.call-update) | async-done | bytes 204816 | tf_op jit(solution)/shard_map/reduce_scatter | solution.py:278
  (256 shorter events, 246.2 us)
Async XLA Ops:
  7.2 127.0 %copy-start = (bf16[2,128,1280]{2,1,0:T(8,128)(2,1)S(1)}, bf16[2,128,1280]{2,1,0:T(8,128)(2,1)}, u32[]{:S(2)}) copy-start(bf16[2,128,1280]{2,1,0:T(8,128)(2,1)} %param.23) | copy-start | bytes 1966084
  7.2 65.8 %all-gather.15.cloned.1.call-start = ((), (), s32[]{:S(2)}) async-start(), calls=%async_computation.6 | async-start | bytes 3379200 | tf_op jit(solution)/shard_map/all_gather | solution.py:175
  7.9 126.2 %all-gather.21.cloned.1.call-start = ((), (), s32[]{:S(2)}) async-start(), calls=%async_computation.9 | async-start | bytes 3379200 | tf_op jit(solution)/shard_map/all_gather | solution.py:176
  8.7 186.6 %all-gather.19.cloned.1.call-start = ((), (), s32[]{:S(2)}) async-start(), calls=%async_computation.8 | async-start | bytes 3379200 | tf_op jit(solution)/shard_map/all_gather | solution.py:174
  9.4 220.2 %all-gather.31.cloned.1.call-start = ((), (), s32[]{:S(2)}) async-start(), calls=%async_computation.14 | async-start | bytes 2949120 | tf_op jit(solution)/shard_map/all_gather | solution.py:43
  54.2 92.1 %copy-start.40 = (bf16[1280]{0:T(1024)(128)(2,1)}, bf16[1280]{0:T(1024)(128)(2,1)S(1)}, u32[]{:S(2)}) copy-start(bf16[1280]{0:T(1024)(128)(2,1)S(1)} %get-tuple-element.289) | copy-start | bytes 7684
  76.4 187.6 %all-gather.33.cloned.1.call-start = ((), (), s32[]{:S(2)}) async-start(), calls=%async_computation.15 | async-start | bytes 2949120 | tf_op jit(solution)/shard_map/all_gather | solution.py:44
  137.5 160.3 %all-gather.17.cloned.1.call-start = ((), (), s32[]{:S(2)}) async-start(), calls=%async_computation.7 | async-start | bytes 2949120 | tf_op jit(solution)/shard_map/all_gather | solution.py:43
  140.9 192.1 %all-gather.23.cloned.1.call-start = ((), (), s32[]{:S(2)}) async-start(), calls=%async_computation.10 | async-start | bytes 2949120 | tf_op jit(solution)/shard_map/all_gather | solution.py:44
  144.2 250.0 %all-gather.25.cloned.1.call-start = ((), (), s32[]{:S(2)}) async-start(), calls=%async_computation.11 | async-start | bytes 3379200 | tf_op jit(solution)/shard_map/all_gather | solution.py:177
  145.0 310.4 %all-gather.27.cloned.1.call-start = ((), (), s32[]{:S(2)}) async-start(), calls=%async_computation.12 | async-start | bytes 3379200 | tf_op jit(solution)/shard_map/all_gather | solution.py:178
  145.7 370.6 %all-gather.29.cloned.1.call-start = ((), (), s32[]{:S(2)}) async-start(), calls=%async_computation.13 | async-start | bytes 3379200 | tf_op jit(solution)/shard_map/all_gather | solution.py:179
  146.3 537.7 %all-gather.39.cloned.1.call-start = ((), (), s32[]{:S(2)}) async-start(), calls=%async_computation.18 | async-start | bytes 2949120 | tf_op jit(solution)/shard_map/all_gather | solution.py:116
  199.8 64.2 %copy-start.26 = (bf16[128,1280]{1,0:T(8,128)(2,1)}, bf16[128,1280]{1,0:T(8,128)(2,1)S(1)}, u32[]{:S(2)}) copy-start(bf16[128,1280]{1,0:T(8,128)(2,1)S(1)} %get-tuple-element.305) | copy-start | bytes 983044
  199.8 484.2 %all-gather.41.cloned.1.call-start = ((), (), s32[]{:S(2)}) async-start(), calls=%async_computation.19 | async-start | bytes 2949120 | tf_op jit(solution)/shard_map/all_gather | solution.py:117
  269.6 3.8 copy-start.8
  354.4 173.0 %copy-start.10 = (f32[128,1280]{1,0:T(8,128)}, f32[128,1280]{1,0:T(8,128)S(1)}, u32[]{:S(2)}) copy-start(f32[128,1280]{1,0:T(8,128)S(1)} %div.48) | copy-start | bytes 1966084
  530.6 189.2 %all-gather.35.cloned.1.call-start = ((), (), s32[]{:S(2)}) async-start(), calls=%async_computation.16 | async-start | bytes 2949120 | tf_op jit(solution)/shard_map/all_gather | solution.py:116
  531.3 188.4 %all-gather.37.cloned.1.call-start = ((), (), s32[]{:S(2)}) async-start(), calls=%async_computation.17 | async-start | bytes 2949120 | tf_op jit(solution)/shard_map/all_gather | solution.py:117
  535.8 6.8 copy-start.23
  535.8 6.8 copy-start.27
  535.8 291.8 %reduce-scatter.7.cloned.1.call-start = ((), (), s32[]{:S(2)}) async-start(), calls=%async_computation.20 | async-start | bytes 6758400 | tf_op jit(solution)/shard_map/reduce_scatter | solution.py:276
  605.2 348.0 %reduce-scatter.13.cloned.1.call-start = ((), (), s32[]{:S(2)}) async-start(), calls=%async_computation.23 | async-start | bytes 6758400 | tf_op jit(solution)/shard_map/reduce_scatter | solution.py:279
  611.3 490.8 %reduce-scatter.15.cloned.1.call-start = ((), (), s32[]{:S(2)}) async-start(), calls=%async_computation.24 | async-start | bytes 6758400 | tf_op jit(solution)/shard_map/reduce_scatter | solution.py:280
  617.3 633.2 %reduce-scatter.17.cloned.1.call-start = ((), (), s32[]{:S(2)}) async-start(), calls=%async_computation.25 | async-start | bytes 6758400 | tf_op jit(solution)/shard_map/reduce_scatter | solution.py:281
  624.4 774.4 %reduce-scatter.9.cloned.1.call-start = ((), (), s32[]{:S(2)}) async-start(), calls=%async_computation.21 | async-start | bytes 6758400 | tf_op jit(solution)/shard_map/reduce_scatter | solution.py:277
  684.0 35.7 %copy-start.24 = (bf16[128,1280]{1,0:T(8,128)(2,1)S(1)}, bf16[128,1280]{1,0:T(8,128)(2,1)}, u32[]{:S(2)}) copy-start(bf16[128,1280]{1,0:T(8,128)(2,1)} %convolution_convert_fusion.5) | copy-start | bytes 983044
  684.0 35.7 %copy-start.25 = (bf16[128,1280]{1,0:T(8,128)(2,1)S(1)}, bf16[128,1280]{1,0:T(8,128)(2,1)}, u32[]{:S(2)}) copy-start(bf16[128,1280]{1,0:T(8,128)(2,1)} %convolution_convert_fusion.4) | copy-start | bytes 983044
  752.4 6.1 copy-start.34
  758.4 788.0 %reduce-scatter.11.cloned.1.call-start = ((), (), s32[]{:S(2)}) async-start(), calls=%async_computation.22 | async-start | bytes 6758400 | tf_op jit(solution)/shard_map/reduce_scatter | solution.py:278
  781.4 43.6 %copy-start.15 = (f32[128,1280]{1,0:T(8,128)S(1)}, f32[128,1280]{1,0:T(8,128)}, u32[]{:S(2)}) copy-start(f32[128,1280]{1,0:T(8,128)} %copy-done.13) | copy-start | bytes 1966084
  781.4 43.6 %copy-start.18 = (f32[128,1280]{1,0:T(8,128)S(1)}, f32[128,1280]{1,0:T(8,128)}, u32[]{:S(2)}) copy-start(f32[128,1280]{1,0:T(8,128)} %get-tuple-element.301) | copy-start | bytes 1966084
  (32 other events, 71.4 us)
Sparse Core Ops, SparseCore 0:
  10.9 62.0 all-gather.14
  75.8 58.2 all-gather.20
  137.0 58.2 all-gather.18
  196.8 32.7 all-gather.30
  231.1 32.8 all-gather.32
  265.5 32.2 all-gather.16
  299.4 33.4 all-gather.22
  335.8 58.3 all-gather.24
  397.0 58.2 all-gather.26
  458.0 58.2 all-gather.28
  518.0 32.7 all-gather.38
  552.3 32.8 all-gather.40
  586.8 32.8 all-gather.34
  621.2 33.7 all-gather.36
  657.7 147.3 reduce-scatter.6
  807.8 145.3 reduce-scatter.12
  955.9 146.0 reduce-scatter.14
  1104.8 145.7 reduce-scatter.16
  1253.4 145.3 reduce-scatter.8
  1401.5 144.7 reduce-scatter.10
where the time goes:
time: 1560 us; the launch traced here: 1550 us
  waiting for transfers between devices  1110 us (71%)
  matrix products  182 us (12%)
  blocking collectives  141 us (9%)
  local copies, waits for them, and re-layouts  83.9 us (5%)
  other arithmetic  19.1 us (1%)
    reduce_scatter x1, waiting for transfers between devices, per_device(): lax.psum_scatter(totals[4], ('dp', 'seq'), scatter_dimension=0, tiled=True)  149 us
    reduce_scatter x1, waiting for transfers between devices, per_device(): lax.psum_scatter(totals[5], ('dp', 'seq'), scatter_dimension=0, tiled=True)  148 us
    reduce_scatter x1, waiting for transfers between devices, per_device(): lax.psum_scatter(totals[1], ('dp', 'seq'), scatter_dimension=0, tiled=True)  148 us
    reduce_scatter x1, waiting for transfers between devices, per_device(): lax.psum_scatter(totals[2], ('dp', 'seq'), scatter_dimension=0, tiled=True)  148 us
    reduce_scatter x1, waiting for transfers between devices, per_device(): lax.psum_scatter(totals[3], ('dp', 'seq'), scatter_dimension=0, tiled=True)  126 us
    unnamed x2, blocking collectives  81.8 us
    all_gather x2, waiting for transfers between devices, attend(): value_piece = lax.all_gather(v_low, 'seq', axis=0, tiled=True)  69.5 us
    all_gather x1, waiting for transfers between devices, per_device(): lax.all_gather(w_value, ('dp', 'seq'), axis=0, tiled=True)  57.7 us
  transfers between devices with their start and end apart: 20, of which 15 were waited for; matrix products, arithmetic and copies ran while one was open for 18% of the time, Pallas kernels for 0%

commit v1 on v0

--- a/solution.py
+++ b/solution.py
@@ -1,15 +1,319 @@
+import functools
 import math
 
 import jax
 import jax.numpy as jnp
 from jax import lax
+from jax.experimental import pallas as pl
+from jax.experimental.pallas import tpu as pltpu
+from jax.sharding import Mesh
 from jax.sharding import PartitionSpec as P
 
 H = 16
-
-
 EPS = 1e-06
 SOFT_BASE = 1.442695
+BF = jnp.bfloat16
+F32 = jnp.float32
+NN = (((1,), (0,)), ((), ()))
+NT = (((1,), (1,)), ((), ()))
+TN = (((0,), (0,)), ((), ()))
+DP = ("y", "x")
+SEQ = ("z", "c")
+ALL = ("y", "x", "z", "c")
+BLOCK = 256
+
+
+def mm(left, right, dims):
+    return lax.dot_general(left, right, dims, preferred_element_type=F32)
+
+
+def forward_kernel(hd, x_ref, gain_ref, w_ref, scale_ref, o_ref, h_ref, kn_ref, vn_ref, qt_ref, kt_ref, ot_ref, lse_ref):
+    length = x_ref.shape[0]
+    cols = w_ref.shape[0] // 3
+    heads = cols // hd
+    step = min(BLOCK, length)
+    w = w_ref[...]
+    gain = gain_ref[...]
+    vt_parts = []
+    for r in range(0, length, step):
+        x = x_ref[r : r + step, :].astype(F32)
+        inv = lax.rsqrt(jnp.mean(x * x, axis=-1, keepdims=True) + EPS)
+        h = (x * inv * gain).astype(BF)
+        h_ref[r : r + step, :] = h
+        qkv = mm(w, h, NT)
+        q = (qkv[:cols] * scale_ref[...]).astype(BF)
+        k = qkv[cols : 2 * cols].astype(BF)
+        v = qkv[2 * cols :].astype(BF)
+        qt_ref[:, r : r + step] = q
+        kt_ref[:, r : r + step] = k
+        kn_ref[r : r + step, :] = qkv[cols : 2 * cols].T.astype(BF)
+        vn_ref[r : r + step, :] = qkv[2 * cols :].T.astype(BF)
+        vt_parts.append(v)
+    vt = jnp.concatenate(vt_parts, axis=1)
+    zero = jnp.zeros((hd, step), BF)
+    causal = lax.broadcasted_iota(jnp.int32, (step, step), 0) <= lax.broadcasted_iota(jnp.int32, (step, step), 1)
+    out_block = o_ref.shape[2]
+    for r in range(0, length, step):
+        n = r + step
+        keys = kn_ref[0:n, :]
+        outs = []
+        for a in range(heads):
+            qh = qt_ref[a * hd : (a + 1) * hd, r:n]
+            qh = jnp.concatenate([qh if b == a else zero for b in range(heads)], axis=0)
+            s = mm(keys, qh, NN)
+            tail = jnp.where(causal, s[r:], -1e30)
+            s = jnp.concatenate([s[:r], tail], axis=0) if r else tail
+            top = jnp.max(s, axis=0, keepdims=True)
+            p = jnp.exp(s - top)
+            total = jnp.sum(p, axis=0, keepdims=True)
+            o = mm(vt[a * hd : (a + 1) * hd, :n], p.astype(BF), NN) / total
+            lse_ref[a : a + 1, r:n] = top + jnp.log(total)
+            outs.append(o)
+        o = jnp.concatenate(outs, axis=0)
+        ot_ref[:, r:n] = o
+        for b in range(r // out_block, n // out_block):
+            o_ref[b] = o[:, b * out_block - r : (b + 1) * out_block - r].astype(BF)
+
+
+def attention_forward(x, gain, w_t, scale, hd, blocks):
+    micro, length, width = x.shape
+    cols = w_t.shape[0] // 3
+    rows = length // blocks
+    step = pl.Squeezed()
+    return pl.pallas_call(
+        functools.partial(forward_kernel, hd),
+        grid=(micro,),
+        in_specs=[
+            pl.BlockSpec((step, length, width), lambda m: (m, 0, 0)),
+            pl.BlockSpec((1, width), lambda m: (0, 0)),
+            pl.BlockSpec((3 * cols, width), lambda m: (0, 0)),
+            pl.BlockSpec((cols, 1), lambda m: (0, 0)),
+        ],
+        out_specs=[
+            pl.BlockSpec((blocks, cols, rows), lambda m: (0, 0, m)),
+            pl.BlockSpec((step, length, width), lambda m: (m, 0, 0)),
+            pl.BlockSpec((step, length, cols), lambda m: (m, 0, 0)),
+            pl.BlockSpec((step, length, cols), lambda m: (m, 0, 0)),
+            pl.BlockSpec((step, cols, length), lambda m: (m, 0, 0)),
+            pl.BlockSpec((step, cols, length), lambda m: (m, 0, 0)),
+            pl.BlockSpec((step, cols, length), lambda m: (m, 0, 0)),
+            pl.BlockSpec((step, 8, length), lambda m: (m, 0, 0)),
+        ],
+        out_shape=[
+            jax.ShapeDtypeStruct((blocks, cols, micro * rows), BF),
+            jax.ShapeDtypeStruct((micro, length, width), BF),
+            jax.ShapeDtypeStruct((micro, length, cols), BF),
+            jax.ShapeDtypeStruct((micro, length, cols), BF),
+            jax.ShapeDtypeStruct((micro, cols, length), BF),
+            jax.ShapeDtypeStruct((micro, cols, length), BF),
+            jax.ShapeDtypeStruct((micro, cols, length), F32),
+            jax.ShapeDtypeStruct((micro, 8, length), F32),
+        ],
+        compiler_params=pltpu.CompilerParams(vmem_limit_bytes=56 << 20),
+        name="attention_forward",
+    )(x, gain, w_t, scale)
+
+
+def backward_kernel(hd, do_ref, kn_ref, vn_ref, qt_ref, kt_ref, ot_ref, lse_ref, scale_ref, g_ref, gs_ref, dk_acc, dv_acc):
+    blocks, cols, rows = do_ref.shape
+    length = blocks * rows
+    heads = cols // hd
+    step = min(BLOCK, length)
+    do = jnp.concatenate([do_ref[b] for b in range(blocks)], axis=1)
+    zero = jnp.zeros((hd, step), BF)
+    causal = lax.broadcasted_iota(jnp.int32, (step, step), 0) <= lax.broadcasted_iota(jnp.int32, (step, step), 1)
+    gs = jnp.zeros((cols, 1), F32)
+    for r in range(length - step, -1, -step):
+        n = r + step
+        keys, values = kn_ref[0:n, :], vn_ref[0:n, :]
+        prod = do[:, r:n].astype(F32) * ot_ref[:, r:n]
+        dqs = []
+        for a in range(heads):
+            lo, hi = a * hd, (a + 1) * hd
+            qh, doh = qt_ref[lo:hi, r:n], do[lo:hi, r:n]
+            q_wide = jnp.concatenate([qh if b == a else zero for b in range(heads)], axis=0)
+            do_wide = jnp.concatenate([doh if b == a else zero for b in range(heads)], axis=0)
+            delta = jnp.sum(prod[lo:hi], axis=0, keepdims=True)
+            s = mm(keys, q_wide, NN) - lse_ref[a : a + 1, r:n]
+            tail = jnp.where(causal, s[r:], -1e30)
+            s = jnp.concatenate([s[:r], tail], axis=0) if r else tail
+            p = jnp.exp(s)
+            dp = mm(values, do_wide, NN)
+            ds = (p * (dp - delta)).astype(BF)
+            p = p.astype(BF)
+            dv = mm(doh, p, NT)
+            dk = mm(qh, ds, NT)
+            if n == length:
+                dv_acc[lo:hi, :] = dv
+                dk_acc[lo:hi, :] = dk
+            else:
+                dv_acc[lo:hi, 0:n] += dv
+                dk_acc[lo:hi, 0:n] += dk
+            dqs.append(mm(kt_ref[lo:hi, 0:n], ds, NN))
+        dq = jnp.concatenate(dqs, axis=0)
+        gs = gs + jnp.sum(dq * qt_ref[:, r:n].astype(F32), axis=1, keepdims=True)
+        dq = (dq * scale_ref[...]).astype(BF)
+        for b in range(r // rows, n // rows):
+            g_ref[b, 0:cols] = dq[:, b * rows - r : (b + 1) * rows - r]
+    for b in range(blocks):
+        g_ref[b, cols : 2 * cols] = dk_acc[:, b * rows : (b + 1) * rows].astype(BF)
+        g_ref[b, 2 * cols : 3 * cols] = dv_acc[:, b * rows : (b + 1) * rows].astype(BF)
+    gs_ref[...] = gs
+
+
+def attention_backward(do, saved, scale, hd):
+    kn, vn, qt, kt, ot, lse = saved
+    micro, length, cols = kn.shape
+    blocks = do.shape[0]
+    rows = length // blocks
+    step = pl.Squeezed()
+    return pl.pallas_call(
+        functools.partial(backward_kernel, hd),
+        grid=(micro,),
+        in_specs=[
+            pl.BlockSpec((blocks, cols, rows), lambda m: (0, 0, m)),
+            pl.BlockSpec((step, length, cols), lambda m: (m, 0, 0)),
+            pl.BlockSpec((step, length, cols), lambda m: (m, 0, 0)),
+            pl.BlockSpec((step, cols, length), lambda m: (m, 0, 0)),
+            pl.BlockSpec((step, cols, length), lambda m: (m, 0, 0)),
+            pl.BlockSpec((step, cols, length), lambda m: (m, 0, 0)),
+            pl.BlockSpec((step, 8, length), lambda m: (m, 0, 0)),
+            pl.BlockSpec((cols, 1), lambda m: (0, 0)),
+        ],
+        out_specs=[
+            pl.BlockSpec((blocks, 3 * cols, rows), lambda m: (0, 0, m)),
+            pl.BlockSpec((step, cols, 1), lambda m: (m, 0, 0)),
+        ],
+        out_shape=[
+            jax.ShapeDtypeStruct((blocks, 3 * cols, micro * rows), BF),
+            jax.ShapeDtypeStruct((micro, cols, 1), F32),
+        ],
+        scratch_shapes=[pltpu.VMEM((cols, length), F32), pltpu.VMEM((cols, length), F32)],
+        compiler_params=pltpu.CompilerParams(vmem_limit_bytes=56 << 20),
+        name="attention_backward",
+    )(do, kn, vn, qt, kt, ot, lse, scale)
+
+
+def exchange(value, axes):
+    return lax.all_to_all(value, axes, split_axis=0, concat_axis=0, tiled=True)
+
+
+def head_parallel(inputs, cotangent, w_query, w_key, w_value, w_out, w_up, w_down, norm_attn, norm_mlp, query_scale):
+    micro, rows, width = inputs.shape
+    n_dp = lax.axis_size(DP)
+    n_seq = lax.axis_size(SEQ)
+    n_all = n_dp * n_seq
+    hd = width // H
+    cols = width // n_seq
+    shard = w_query.shape[0]
+    seq_index = lax.axis_index(SEQ)
+    tokens = micro * rows
+
+    x_all = lax.all_gather(inputs, SEQ, axis=1, tiled=True)
+    pad = -(3 * shard + 1) % 128 + 1
+    pieces = [w.T.reshape(n_seq, cols, shard) for w in (w_query, w_key, w_value)]
+    vectors = jnp.concatenate([norm_attn, norm_mlp, query_scale])
+    side = jnp.zeros((cols, pad), BF).at[: 3 * shard, 0].set(vectors)
+    packed = jnp.concatenate(pieces + [jnp.broadcast_to(side, (n_seq, cols, pad))], axis=2)
+    mine = lax.all_gather(exchange(packed, SEQ), DP, axis=0, tiled=True)
+    w_t = jnp.concatenate(
+        [
+            jnp.transpose(mine[:, :, i * shard : (i + 1) * shard], (1, 0, 2)).reshape(cols, width)
+            for i in range(3)
+        ],
+        axis=0,
+    )
+    vectors = mine[:, : 3 * shard, 3 * shard].astype(F32)
+    gain_attn = vectors[:, :shard].reshape(1, width)
+    gain_mlp = vectors[:, shard : 2 * shard].reshape(1, width)
+    param = lax.dynamic_slice(vectors[:, 2 * shard :].reshape(width, 1), (seq_index * cols, 0), (cols, 1))
+    factor = SOFT_BASE / math.sqrt(hd)
+    scale = jax.nn.softplus(param) * factor
+
+    def whole(*shards):
+        parts = lax.all_gather(jnp.stack(shards), ALL, axis=0, tiled=False)
+        return [parts[:, i].reshape(width, width) for i in range(len(shards))]
+
+    full_out, full_up, full_down = whole(w_out, w_up, w_down)
+    full_query, full_key, full_value = whole(w_query, w_key, w_value)
+
+    o, h_all, kn, vn, qt, kt, ot, lse = attention_forward(x_all, gain_attn, w_t, scale, hd, n_seq)
+    attn_t = exchange(o, SEQ).reshape(width, tokens)
+
+    xf = inputs.reshape(tokens, width).astype(F32)
+    dy_low = cotangent.reshape(tokens, width)
+    dy = dy_low.astype(F32)
+    resid = xf + mm(attn_t, full_out, TN)
+    inv_m = lax.rsqrt(jnp.mean(resid * resid, axis=-1, keepdims=True) + EPS)
+    normed = resid * inv_m
+    h_mlp = (normed * gain_mlp).astype(BF)
+    up = mm(h_mlp, full_up, NN)
+    sig = jax.nn.sigmoid(up)
+    act = (up * sig).astype(BF)
+    output = (resid + mm(act, full_down, NN)).astype(BF)
+    d_act = mm(dy_low, full_down, NT)
+    d_up = (d_act * sig * (1.0 + up * (1.0 - sig))).astype(BF)
+    d_hmlp = mm(d_up, full_up, NT)
+    g = d_hmlp * gain_mlp
+    d_resid = dy + inv_m * (g - normed * jnp.mean(g * normed, axis=-1, keepdims=True))
+    dr_low = d_resid.astype(BF)
+    d_mixed_t = mm(full_out, dr_low, NT).astype(BF)
+    do = exchange(d_mixed_t.reshape(n_seq, cols, tokens), SEQ)
+
+    grads = [mm(attn_t, dr_low, NN), mm(h_mlp, d_up, TN), mm(act, dy_low, TN)]
+    grads = jnp.concatenate([g.astype(BF).reshape(n_all, 1, shard, width) for g in grads], axis=1)
+    reduced = lax.psum_scatter(grads.reshape(n_all * 3 * shard, width), ALL, scatter_dimension=0, tiled=True)
+    reduced = reduced.astype(F32).reshape(3, shard, width)
+    grad_out, grad_up, grad_down = reduced[0], reduced[1], reduced[2]
+
+    d_heads, gs = attention_backward(do, (kn, vn, qt, kt, ot, lse), scale, hd)
+    d_tokens = exchange(d_heads, SEQ)
+    dq_t = d_tokens[:, :cols].reshape(width, tokens)
+    dk_t = d_tokens[:, cols : 2 * cols].reshape(width, tokens)
+    dv_t = d_tokens[:, 2 * cols :].reshape(width, tokens)
+    d_hattn = mm(dq_t, full_query, (((0,), (1,)), ((), ())))
+    d_hattn = d_hattn + mm(dk_t, full_key, (((0,), (1,)), ((), ())))
+    d_hattn = d_hattn + mm(dv_t, full_value, (((0,), (1,)), ((), ())))
+    inv_a = lax.rsqrt(jnp.mean(xf * xf, axis=-1, keepdims=True) + EPS)
+    m = xf * inv_a
+    e = d_hattn * gain_attn
+    input_grad = d_resid + inv_a * (e - m * jnp.mean(e * m, axis=-1, keepdims=True))
+
+    gs = jnp.sum(gs, axis=0) / scale * jax.nn.sigmoid(param) * factor
+    h_blocks = h_all.reshape(micro, n_seq, rows, width)
+    d_blocks = d_heads.reshape(n_seq, 3 * cols, micro, rows)
+    part = jnp.einsum("msrf,scmr->fc", h_blocks, d_blocks, preferred_element_type=F32).astype(BF)
+    part = part.reshape(n_dp, width // n_dp, 3 * cols)
+    extra = jnp.zeros((n_dp, 16, 3 * cols), BF).at[:, 0, :cols].set(gs[:, 0].astype(BF))
+    part = exchange(jnp.concatenate([part, extra], axis=1), DP)
+    part = jnp.sum(part.astype(F32), axis=0)
+    last = width // n_dp
+    part_w = part[:last].astype(BF).reshape(n_seq, shard, 3 * cols)
+    part_s = jnp.broadcast_to(part[last : last + 8].astype(BF), (n_seq, 8, 3 * cols))
+    part = exchange(jnp.concatenate([part_w, part_s], axis=1), SEQ).astype(F32)
+    grad_query, grad_key, grad_value = [
+        jnp.transpose(part[:, :shard, i * cols : (i + 1) * cols], (1, 0, 2)).reshape(shard, width) for i in range(3)
+    ]
+    first = (lax.axis_index(DP) * n_seq + seq_index) * shard
+    grad_scale = lax.dynamic_slice(part[:, shard, :cols].reshape(width), (first,), (shard,))
+    low = [w.astype(F32) for w in (w_query, w_key, w_value, w_up)]
+    grad_gain_attn = (
+        jnp.sum(low[0] * grad_query + low[1] * grad_key + low[2] * grad_value, axis=1) / norm_attn.astype(F32)
+    )
+    grad_gain_mlp = jnp.sum(low[3] * grad_up, axis=1) / norm_mlp.astype(F32)
+    return (
+        output.reshape(micro, rows, width),
+        input_grad.reshape(micro, rows, width),
+        grad_query,
+        grad_key,
+        grad_value,
+        grad_out,
+        grad_up,
+        grad_down,
+        grad_gain_attn,
+        grad_gain_mlp,
+        grad_scale,
+    )
 
 
 def weight_outer(left, right):
@@ -149,7 +453,7 @@
     )
 
 
-def per_device(
+def sequence_parallel(
     inputs,
     cotangent,
     w_query,
@@ -299,35 +603,16 @@
 
 
 def solution(mesh):
-    placed = (
-        P("dp", "seq", None),
-        P("dp", "seq", None),
-        P(("dp", "seq"), None),
-        P(("dp", "seq"), None),
-        P(("dp", "seq"), None),
-        P(("dp", "seq"), None),
-        P(("dp", "seq"), None),
-        P(("dp", "seq"), None),
-        P(("dp", "seq")),
-        P(("dp", "seq")),
-        P(("dp", "seq")),
-    )
-    return jax.shard_map(
-        per_device,
-        mesh=mesh,
-        in_specs=placed,
-        out_specs=(
-            P("dp", "seq", None),
-            P("dp", "seq", None),
-            P(("dp", "seq"), None),
-            P(("dp", "seq"), None),
-            P(("dp", "seq"), None),
-            P(("dp", "seq"), None),
-            P(("dp", "seq"), None),
-            P(("dp", "seq"), None),
-            P(("dp", "seq")),
-            P(("dp", "seq")),
-            P(("dp", "seq")),
-        ),
-        check_vma=False,
-    )
+    n_dp, n_seq = mesh.devices.shape
+    if H % n_seq:
+        axes, inner, over = mesh, sequence_parallel, (("dp",), ("seq",))
+    else:
+        core = 2 if n_seq % 2 == 0 else 1
+        wide = 2 if n_dp % 2 == 0 else 1
+        axes = Mesh(mesh.devices.reshape(n_dp // wide, wide, n_seq // core, core), ALL)
+        inner, over = head_parallel, (DP, SEQ)
+    block = P(*over, None)
+    matrix = P(over[0] + over[1], None)
+    vector = P(over[0] + over[1])
+    placed = (block,) * 2 + (matrix,) * 6 + (vector,) * 3
+    return jax.shard_map(inner, mesh=axes, in_specs=placed, out_specs=placed, check_vma=False)

time: 1560 us -> 476 us (0.31)
  waiting for transfers between devices: 1110 us -> 248 us
  matrix products: 182 us -> 28.2 us
  blocking collectives: 141 us -> 79.8 us
  local copies, waits for them, and re-layouts: 83.9 us -> 51.6 us
  Pallas kernels: 0 us -> 25.4 us
    reduce_scatter x6 -> x1, waiting for transfers between devices: 719 us -> 52.4 us  [head_parallel(): lax.psum_scatter(grads.reshape(n_all * 3 * shard, width), ALL, scatter_di...]
    all_gather x14 -> x4, waiting for transfers between devices: 387 us -> 153 us  [the longest x2 70.4 us: whole(): parts = lax.all_gather(jnp.stack(shards), ALL, axis=0, tiled=False)]
    dot_general x50 -> x13, matrix products: 182 us -> 28.2 us  [the longest x12 22.4 us: mm(): return lax.dot_general(left, right, dims, preferred_element_type=F32)]
    unnamed x2 -> x0, blocking collectives: 81.8 us -> none
    all_to_all x0 -> x4, blocking collectives: none -> 79.8 us  [exchange(): return lax.all_to_all(value, axes, split_axis=0, concat_axis=0, tiled=True)]
    all_gather x4 -> x0, blocking collectives: 59.5 us -> none  [the longest x2 30 us: per_device(): lax.all_gather(row_delta, 'seq', axis=1, tiled=True)]
    another operation x18 -> x1, local copies, waits for them, and re-layouts: 55.9 us -> 0.07 us  [head_parallel(): part[:, shard, :cols].reshape(width)]
    all_to_all x0 -> x2, waiting for transfers between devices: none -> 41.9 us  [exchange(): return lax.all_to_all(value, axes, split_axis=0, concat_axis=0, tiled=True)]
  transfers between devices with their start and end apart: 20 -> 7, of which waited for: 15 -> 5; matrix products, arithmetic and copies ran while one was open for 18% -> 18% of each run, Pallas kernels for 0% -> 5%
where the time goes in v1:
time: 476 us; the launch traced here: 474 us
  waiting for transfers between devices  248 us (52%)
  blocking collectives  79.8 us (17%)
  local copies, waits for them, and re-layouts  51.6 us (11%)
  matrix products  28.2 us (6%)
  Pallas kernels  25.4 us (5%)
  other arithmetic  18.1 us (4%)
  between operations  14.3 us (3%)
  starting transfers between devices  9.46 us (2%)
    all_to_all x4, blocking collectives, exchange(): return lax.all_to_all(value, axes, split_axis=0, concat_axis=0, tiled=True)  79.8 us
    all_gather x2, waiting for transfers between devices, whole(): parts = lax.all_gather(jnp.stack(shards), ALL, axis=0, tiled=False)  70.4 us
    reduce_scatter x1, waiting for transfers between devices, head_parallel(): lax.psum_scatter(grads.reshape(n_all * 3 * shard, width), ALL, scatter_di...  52.4 us
    all_gather x1, waiting for transfers between devices, head_parallel(): x_all = lax.all_gather(inputs, SEQ, axis=1, tiled=True)  50.4 us
    all_to_all x2, waiting for transfers between devices, exchange(): return lax.all_to_all(value, axes, split_axis=0, concat_axis=0, tiled=True)  41.9 us
    all_gather x1, waiting for transfers between devices, head_parallel(): mine = lax.all_gather(exchange(packed, SEQ), DP, axis=0, tiled=True)  31.7 us
    dot_general x12, matrix products, mm(): return lax.dot_general(left, right, dims, preferred_element_type=F32)  22.4 us
    pallas_call x1, Pallas kernels, attention_forward(): pl.pallas_call(functools.partial(forward_kernel, hd), grid=(micro,), in_s...  14.4 us
  transfers between devices with their start and end apart: 7, of which 5 were waited for; matrix products, arithmetic and copies ran while one was open for 18% of the time, Pallas kernels for 5%

profile of v1, /device:TPU:0, one launch (start us, length us, event | category | flops | bytes accessed | tf_op | source)
XLA Modules:
  0.0 474.4 jit_solution(11033744472218189106)
XLA Ops:
  12.0 17.4 %all_to_all.30 = bf16[8,160,128]{2,1,0:T(8,128)(2,1)S(1)} all-to-all(bf16[8,160,128]{2,1,0:T(8,128)(2,1)S(1)} %pad_maximum_fusion.4), channel_id=1, replica_groups=mesh['y'=2,'x'=2,'z'=4,'c'=2] {'z','c'}, dimensions={0} | all-to-all | bytes 655360 | tf_op jit(solution)/shard_map/all_to_all | solution.py:198
  33.2 31.7 %all-gather.9.cloned.1.call-done = bf16[32,160,128]{1,0,2:T(8,128)(2,1)} async-done(((bf16[8,160,128]{1,0,2:T(8,128)(2,1)}), bf16[32,160,128]{1,0,2:T(8,128)(2,1)}) %all-gather.9.cloned.1.call-update) | async-done | bytes 1310736 | tf_op jit(solution)/shard_map/all_gather | solution.py:218
  65.9 1.9 slice_bitcast_fusion.2
  72.1 50.4 %all-gather.7.cloned.1.call-done.x_ref = bf16[2,1024,1280]{2,1,0:T(8,128)(2,1)} async-done(((bf16[2,128,1280]{2,1,0:T(8,128)(2,1)}), bf16[2,1024,1280]{2,1,0:T(8,128)(2,1)}) %all-gather.7.cloned.1.call-update) | async-done | bytes 5242896 | tf_op jit(solution)/shard_map/all_gather | solution.py:212
  122.5 14.4 %attention_forward.1 = (bf16[8,160,256]{2,1,0:T(8,128)(2,1)}, bf16[2,1024,1280]{2,1,0:T(8,128)(2,1)}, bf16[2,1024,160]{2,1,0:T(8,128)(2,1)}, bf16[2,1024,160]{2,...) custom-call(bf16[2,1024,1280]{2,1,0:T(8,128)(2,1)} %all-gather.7.clo, ...), custom_call_target="tpu_custom_call" | custom-call | tf_op jit(solution)/shard_map/attention_forward/pallas_call | solution.py:83
  137.0 4.2 all-to-all-start.1
  141.5 70.4 %all-gather.11.cloned.1.call-done = bf16[96,40,1280]{2,1,0:T(8,128)(2,1)} async-done(((bf16[3,40,1280]{2,1,0:T(8,128)(2,1)}), bf16[96,40,1280]{2,1,0:T(8,128)(2,1)}) %all-gather.11.cloned.1.call-update) | async-done | bytes 9830416 | tf_op jit(solution)/shard_map/all_gather | solution.py:234
  211.9 6.2 %fusion.15 = (bf16[32,1,40,1280]{3,2,1,0:T(8,128)(2,1)S(1)}, bf16[32,1,40,1280]{3,2,1,0:T(8,128)(2,1)}, bf16[32,1,40,1280]{3,2,1,0:T(8,128)(2,1)}) fusion(bf16[32,3,40,1280]{3,2,1,0:T(8,128)(2,1)} %bitcast.117), kind=kLoop, calls=%fused_computation.62 | loop fusion | bytes 19660800 | tf_op jit(solution)/shard_map/slice | solution.py:235
  218.1 3.4 multiply_reduce_fusion.3
  222.7 1.8 copy-done.8
  227.4 2.6 convolution_convert_fusion.2
  232.5 4.6 pad_maximum_fusion
  237.0 8.3 %copy.115 = bf16[32,3,40,1280]{3,2,1,0:T(8,128)(2,1)} copy(bf16[32,3,40,1280]{3,2,0,1:T(8,128)(2,1)} %pad_maximum_fusion) | data formatting | bytes 19660800 | tf_op jit(solution)/shard_map/concatenate | solution.py:264
  245.3 3.0 convolution_convert_fusion.3
  248.3 25.6 %all_to_all.31.do_ref = bf16[8,160,256]{2,1,0:T(8,128)(2,1)} all-to-all(bf16[8,160,256]{2,1,0:T(8,128)(2,1)S(1)} %bitcast.141), channel_id=1, replica_groups=mesh['y'=2,'x'=2,'z'=4,'c'=2] {'z','c'}, dimensions={0} | all-to-all | bytes 1310720 | tf_op jit(solution)/shard_map/all_to_all | solution.py:198
  273.8 10.9 %attention_backward.1 = (bf16[8,480,256]{2,1,0:T(8,128)(2,1)}, f32[2,160,1]{2,1,0:T(8,128)}) custom-call(bf16[8,160,256]{2,1,0:T(8,128)(2,1)} %all_to_all.31.do_ref, bf16[2,1024,160]{2,1,0:T(8,128)(2,1)} %get-tuple-element.46.kn_ref, bf16[2,1024,160]{2,1,0:T(8,128)(2,1)} %get-tuple-element.47.vn_ref, bf16[2,160,1024]{2,1,0:T(8,128)(2,1)} %get-tuple-element.48.qt_ref, ...), custom_call_target="tpu_custom_call" | custom-call | tf_op jit(solution)/shard_map/attention_backward/pallas_call | solution.py:170
  284.8 5.8 %fusion = bf16[1280,480]{0,1:T(8,128)(2,1)S(1)} fusion(bf16[2,8,128,1280]{3,2,1,0:T(8,128)(2,1)} %bitcast.149, bf16[8,480,256]{2,1,0:T(8,128)(2,1)} %get-tuple-element.52), kind=kOutput, calls=%fused_computation.5 | convolution fusion | flops 2517196800 | bytes 8437760 | tf_op jit(solution)/shard_map/msrf,scmr->fc/dot_general | solution.py:285
  293.0 20.4 %all_to_all.32 = bf16[4,336,480]{2,1,0:T(8,128)(2,1)S(1)} all-to-all(bf16[4,336,480]{2,1,0:T(8,128)(2,1)S(1)} %pad_maximum_fusion.1), channel_id=1, replica_groups=mesh['y'=2,'x'=2,'z'=4,'c'=2] {'y','x'}, dimensions={0} | all-to-all | bytes 2580480 | tf_op jit(solution)/shard_map/all_to_all | solution.py:198
  313.9 16.5 %all_to_all.33 = bf16[8,48,480]{2,1,0:T(8,128)(2,1)} all-to-all(bf16[8,48,480]{2,1,0:T(8,128)(2,1)S(1)} %pad_maximum_fusion.3), channel_id=1, replica_groups=mesh['y'=2,'x'=2,'z'=4,'c'=2] {'z','c'}, dimensions={0} | all-to-all | bytes 737280 | tf_op jit(solution)/shard_map/all_to_all | solution.py:198
  330.4 4.9 %all-to-all-start.3 = ((bf16[8,480,256]{2,1,0:T(8,128)(2,1)}), bf16[8,480,256]{2,1,0:T(8,128)(2,1)}, u32[]{:S(2)}, u32[]{:S(2)}) async-start(bf16[8,480,256]{2,1,0:T(8,128)(2,1)} %get-tuple-element.52), calls=%async_computation.3 | async-start | bytes 3932160 | tf_op jit(solution)/shard_map/all_to_all | solution.py:198
  335.6 4.1 fusion.5
  339.7 7.3 %fusion.14 = (bf16[32,1,40,1280]{3,2,1,0:T(8,128)(2,1)S(1)}, bf16[32,1,40,1280]{3,2,1,0:T(8,128)(2,1)}, bf16[32,1,40,1280]{3,2,1,0:T(8,128)(2,1)}) fusion(bf16[32,3,40,1280]{3,2,1,0:T(8,128)(2,1)} %bitcast.116), kind=kLoop, calls=%fused_computation.61 | loop fusion | bytes 19660800 | tf_op jit(solution)/shard_map/slice | solution.py:235
  349.9 1.8 reshape.248
  351.8 1.8 copy.113
  353.6 1.8 reshape.249
  355.4 1.8 copy.114
  357.2 1.8 reshape.250
  360.5 1.5 add_reduce_fusion
  362.5 41.9 %all-to-all-done.3 = bf16[8,480,256]{2,1,0:T(8,128)(2,1)} async-done(((bf16[8,480,256]{2,1,0:T(8,128)(2,1)}), bf16[8,480,256]{2,1,0:T(8,128)(2,1)}, u32[]{:S(2)}, u32[]{:S(2)}) %all-to-all-start.3) | async-done | bytes 1966112 | tf_op jit(solution)/shard_map/all_to_all | solution.py:198
  404.4 1.8 fusion.16
  413.0 52.4 %reduce-scatter.2.cloned.1.call-done = bf16[120,1280]{1,0:T(8,128)(2,1)} async-done(((bf16[3840,1280]{1,0:T(8,128)(2,1)}), bf16[120,1280]{1,0:T(8,128)(2,1)}) %reduce-scatter.2.cloned.1.call-update) | async-done | bytes 307216 | tf_op jit(solution)/shard_map/reduce_scatter | solution.py:265
  465.4 1.9 multiply_reduce_fusion.4
  (122 shorter events, 35.9 us)
Async XLA Ops:
  7.2 57.7 %all-gather.9.cloned.1.call-start = ((), (), s32[]{:S(2)}) async-start(), calls=%async_computation.8 | async-start | bytes 2621440 | tf_op jit(solution)/shard_map/all_gather | solution.py:218
  12.0 19.5 %copy-start.18 = (bf16[40,1280]{1,0:T(8,128)(2,1)S(1)}, bf16[40,1280]{1,0:T(8,128)(2,1)}, u32[]{:S(2)}) copy-start(bf16[40,1280]{1,0:T(8,128)(2,1)} %param.21) | copy-start | bytes 307204
  12.0 19.5 %copy-start.21 = (bf16[40,1280]{1,0:T(8,128)(2,1)S(1)}, bf16[40,1280]{1,0:T(8,128)(2,1)}, u32[]{:S(2)}) copy-start(bf16[40,1280]{1,0:T(8,128)(2,1)} %param.22) | copy-start | bytes 307204
  12.0 19.5 %copy-start.22 = (bf16[40,1280]{1,0:T(8,128)(2,1)S(1)}, bf16[40,1280]{1,0:T(8,128)(2,1)}, u32[]{:S(2)}) copy-start(bf16[40,1280]{1,0:T(8,128)(2,1)} %param.20) | copy-start | bytes 307204
  29.4 2.9 copy-start.14
  29.4 2.9 copy-start.15
  29.4 2.9 copy-start.16
  30.7 91.9 %all-gather.7.cloned.1.call-start = ((), (), s32[]{:S(2)}) async-start(), calls=%async_computation.7 | async-start | bytes 5898240 | tf_op jit(solution)/shard_map/all_gather | solution.py:212
  31.4 180.5 %all-gather.11.cloned.1.call-start = ((), (), s32[]{:S(2)}) async-start(), calls=%async_computation.10 | async-start | bytes 10137600 | tf_op jit(solution)/shard_map/all_gather | solution.py:234
  32.3 307.5 %all-gather.13.cloned.1.call-start = ((), (), s32[]{:S(2)}) async-start(), calls=%async_computation.11 | async-start | bytes 10137600 | tf_op jit(solution)/shard_map/all_gather | solution.py:234
  65.9 4.3 copy-start.13
  137.0 81.1 %all-to-all-start.1 = ((bf16[8,160,256]{2,1,0:T(8,128)(2,1)}), bf16[8,160,256]{2,1,0:T(8,128)(2,1)}, u32[]{:S(2)}, u32[]{:S(2)}) async-start(bf16[8,160,256]{2,1,0:T(8,128)(2,1)} %get-tuple-element.45), calls=%async_computation.1 | async-start | bytes 1310720 | tf_op jit(solution)/shard_map/all_to_all | solution.py:198
  141.2 324.2 %reduce-scatter.2.cloned.1.call-start = ((), (), s32[]{:S(2)}) async-start(), calls=%async_computation.9 | async-start | bytes 10137600 | tf_op jit(solution)/shard_map/reduce_scatter | solution.py:265
  221.5 8.4 %copy-start = (f32[256,1280]{1,0:T(8,128)}, f32[256,1280]{1,0:T(8,128)S(1)}, u32[]{:S(2)}) copy-start(f32[256,1280]{1,0:T(8,128)S(1)} %get-tuple-element.78) | copy-start | bytes 3932164
  221.6 2.9 copy-start.8
  221.6 3.1 copy-start.17
  222.7 8.4 %copy-start.11 = (f32[256,1280]{1,0:T(8,128)}, f32[256,1280]{1,0:T(8,128)S(1)}, u32[]{:S(2)}) copy-start(f32[256,1280]{1,0:T(8,128)S(1)} %fusion.13) | copy-start | bytes 3932164
  227.3 17.9 %copy-start.3 = (f32[256,1280]{1,0:T(8,128)}, f32[256,1280]{1,0:T(8,128)S(1)}, u32[]{:S(2)}) copy-start(f32[256,1280]{1,0:T(8,128)S(1)} %multiply_add_fusion.1) | copy-start | bytes 3932164
  290.6 0.9 copy-start.20
  330.4 4.9 %copy-start.5 = (bf16[2,128,1280]{2,1,0:T(8,128)(2,1)S(1)}, bf16[2,128,1280]{2,1,0:T(8,128)(2,1)}, u32[]{:S(2)}) copy-start(bf16[2,128,1280]{2,1,0:T(8,128)(2,1)} %param.15) | copy-start | bytes 1966084
  330.4 5.2 %copy-start.1 = (f32[256,1280]{1,0:T(8,128)S(1)}, f32[256,1280]{1,0:T(8,128)}, u32[]{:S(2)}) copy-start(f32[256,1280]{1,0:T(8,128)} %copy-done) | copy-start | bytes 3932164
  330.4 5.2 %copy-start.12 = (f32[256,1280]{1,0:T(8,128)S(1)}, f32[256,1280]{1,0:T(8,128)}, u32[]{:S(2)}) copy-start(f32[256,1280]{1,0:T(8,128)} %copy-done.11) | copy-start | bytes 3932164
  330.4 74.0 %all-to-all-start.3 = ((bf16[8,480,256]{2,1,0:T(8,128)(2,1)}), bf16[8,480,256]{2,1,0:T(8,128)(2,1)}, u32[]{:S(2)}, u32[]{:S(2)}) async-start(bf16[8,480,256]{2,1,0:T(8,128)(2,1)} %get-tuple-element.52), calls=%async_computation.3 | async-start | bytes 3932160 | tf_op jit(solution)/shard_map/all_to_all | solution.py:198
  339.7 7.3 %copy-start.10 = (bf16[8,48,480]{2,1,0:T(8,128)(2,1)S(1)}, bf16[8,48,480]{2,1,0:T(8,128)(2,1)}, u32[]{:S(2)}) copy-start(bf16[8,48,480]{2,1,0:T(8,128)(2,1)} %all_to_all.33) | copy-start | bytes 1105924
  347.1 0.9 copy-start.7
  353.6 8.4 %copy-start.23 = (bf16[40]{0:T(256)(128)(2,1)S(1)}, bf16[40]{0:T(256)(128)(2,1)}, u32[]{:S(2)}) copy-start(bf16[40]{0:T(256)(128)(2,1)} %param.23) | copy-start | bytes 244
  404.4 2.7 copy-start.9
  407.1 2.1 copy-start.2
  409.2 1.1 copy-start.6
  410.3 1.3 copy-start.4
  411.6 53.7 %copy-start.19 = (bf16[40,1280]{1,0:T(8,128)(2,1)S(1)}, bf16[40,1280]{1,0:T(8,128)(2,1)}, u32[]{:S(2)}) copy-start(bf16[40,1280]{1,0:T(8,128)(2,1)} %param.21) | copy-start | bytes 307204
  413.0 54.3 %copy-start.24 = (bf16[40]{0:T(256)(128)(2,1)S(1)}, bf16[40]{0:T(256)(128)(2,1)}, u32[]{:S(2)}) copy-start(bf16[40]{0:T(256)(128)(2,1)} %param.24) | copy-start | bytes 244
Sparse Core Ops, SparseCore 0:
  30.8 34.0 all-gather.8
  66.5 55.9 all-gather.6
  125.6 86.2 all-gather.10
  214.8 89.0 all-gather.12
  309.7 155.6 reduce-scatter.1
